TPU v7x, 512 devices: a whole 4x8x8 slice. The times are simulated.
512 devices in a mesh: pool: 32 (over z, x), tp: 16 (over y, core).
Axes of the slice: x: 4, y: 8, z: 8, core: 2. Of those that a mesh axis runs over, the one named last changes fastest.
Arguments:
- activations: bfloat16 [2, 256, 8192], P(None, None, 'tp'), may hold values from -6 to 6
- gate_matrix: bfloat16 [8192, 28672], P('tp', 'pool'), may hold values from -0.0625 to 0.0625
- up_weight: bfloat16 [8192, 28672], P('tp', 'pool'), may hold values from -0.0625 to 0.0625
- down_matrix: bfloat16 [28672, 8192], P('pool', 'tp'), may hold values from -0.03125 to 0.03125
- shrink_pages: bfloat16 [128, 64, 8192], P('pool', None, 'tp'), may hold values from -0.0625 to 0.0625
- expand_pages: bfloat16 [128, 64, 28672], P('pool', 'tp'), may hold values from -0.75 to 0.75
- row_adapter: int32 [2, 256], replicated, may hold values from 0 to 127, as said below
- page_table: int32 [128], replicated, may hold values from 0 to 127, as said below
Outputs:
- layer_out: bfloat16 [2, 256, 8192], P(None, None, 'tp')
Inputs may be any that keep to these rules, and one draw needn't show every extreme that they name: `row_adapter`: in each micro-batch, the rows use at most 1 distinct adapter among those whose pages have the same owner, the owner of page g being g // 4 (so a micro-batch may use up to 32 adapters, one per owner). A permutation: adapter a is stored at page page_table[a].
All inputs are finite; a program needn't handle non-finite values.
Results may differ from a plain program's by a relative error of at most 0.0057.
Values may be sent and summed in bfloat16 or wider, within the bound.
A program may use at most 64 MiB of HBM per device.

v0:
```python
import functools

import jax
import jax.numpy as jnp
from jax import lax
from jax.sharding import Mesh
from jax.sharding import PartitionSpec as P

CAP = 1
POOL = ("pool_0", "pool_1")


adapter_scale = 2.0


def in_blocks(value, dim, size):
    before, after = (value.shape[:dim], value.shape[dim + 1 :])
    return jnp.moveaxis(value.reshape(*before, size, -1, *after), dim, 0)


def sum_at_owner(value, axis, dim):
    size = lax.axis_size(axis)
    pieces = lax.all_to_all(in_blocks(value, dim, size), axis, 0, 0, tiled=True)
    return jnp.sum(pieces, axis=0)


def copy_for_each(value, axis):
    copies = jnp.broadcast_to(value, (lax.axis_size(axis), *value.shape))
    return lax.all_to_all(copies, axis, split_axis=0, concat_axis=0, tiled=True)


def over_copies(value, axis):
    everything = copy_for_each(value, axis)
    return jnp.sum(everything, axis=0)


def by_axis(value, axes):
    return functools.reduce(lax.psum, axes, value)


def on_device(
    activations,
    gate_matrix,
    up_weight,
    down_matrix,
    shrink_pages,
    expand_pages,
    row_adapter,
    page_table,
):
    pool_count = lax.axis_size(POOL)
    pool_index = lax.axis_index(POOL)
    batches, row_count, local_width = activations.shape
    page_count = shrink_pages.shape[0]
    rank_local = expand_pages.shape[1]
    hidden_local = gate_matrix.shape[1]
    adapter_total = page_table.shape[0]
    catalog = jnp.arange(adapter_total, dtype=jnp.int32)
    page_of_row = jnp.sum(jnp.where(row_adapter[:, :, None] == catalog, page_table, 0), axis=2)
    groups = [(batch_index, batch_index + 1) for batch_index in range(batches)]
    outputs = []
    for group_start, group_stop in groups:
        group_size = group_stop - group_start
        rows_in = activations[group_start:group_stop].reshape(group_size * row_count, local_width)
        pages_in = page_of_row[group_start:group_stop]
        row_pages = pages_in.reshape(-1)
        row_owner = row_pages // page_count
        row_local = row_pages % page_count
        row_total = group_size * row_count
        projected = jnp.einsum(
            "nd,prd->npr", rows_in, shrink_pages, preferred_element_type=jnp.float32
        )
        owned_here = (row_owner == pool_index)[:, None] & (
            row_local[:, None] == jnp.arange(page_count, dtype=jnp.int32)
        )
        shrink_part = jnp.sum(jnp.where(owned_here[:, :, None], projected, 0.0), axis=1)
        rank_share = sum_at_owner(shrink_part, "tp", 1)
        shrink_mine = over_copies(rank_share, POOL).astype(jnp.bfloat16)
        page_used = jnp.any(pages_in[:, :, None] == catalog, axis=1)
        page_order = jnp.cumsum(page_used.astype(jnp.int32), axis=1) - 1
        owner_order = (
            page_order.reshape(group_size, pool_count, page_count)
            - lax.dynamic_index_in_dim(page_order.reshape(group_size, pool_count, page_count), 0, 2)
            + page_used.reshape(group_size, pool_count, page_count)[:, :, :1].astype(jnp.int32)
            - 1
        )
        owned_used = lax.dynamic_index_in_dim(
            page_used.reshape(group_size, pool_count, page_count), pool_index, 1, keepdims=False
        )
        owned_order = lax.dynamic_index_in_dim(owner_order, pool_index, 1, keepdims=False)
        hit_table = owned_used[:, :, None] & (
            owned_order[:, :, None] == jnp.arange(CAP, dtype=jnp.int32)
        )
        chosen = jnp.sum(
            jnp.where(hit_table, jnp.arange(page_count, dtype=jnp.int32)[None, :, None], 0), axis=1
        )
        outgoing = jnp.take(expand_pages, chosen.reshape(-1), axis=0)
        outgoing = outgoing.reshape(group_size * CAP, rank_local, pool_count, hidden_local)
        received = lax.all_to_all(outgoing, POOL, split_axis=2, concat_axis=0, tiled=True)
        blocks_mat = received.reshape(pool_count * group_size * CAP * rank_local, hidden_local)
        slot_total = pool_count * group_size * CAP
        flat_order = owner_order.reshape(group_size, adapter_total)
        row_order = jnp.sum(
            jnp.where(pages_in[:, :, None] == catalog, flat_order[:, None, :], 0), axis=2
        )
        batch_of_row = lax.broadcasted_iota(jnp.int32, (group_size, row_count), 0)
        slot_of_row = (
            (pages_in // page_count * group_size + batch_of_row) * CAP + row_order
        ).reshape(-1)
        onehot = slot_of_row[:, None] == jnp.arange(slot_total, dtype=jnp.int32)
        wide_rows = jnp.where(
            onehot[:, :, None], shrink_mine[:, None, :], jnp.zeros((), jnp.bfloat16)
        )
        wide_rows = wide_rows.reshape(row_total, slot_total * rank_local)
        gate_term = jnp.dot(rows_in, gate_matrix, preferred_element_type=jnp.float32)
        up_product = jnp.dot(rows_in, up_weight, preferred_element_type=jnp.float32)
        up_product = up_product + adapter_scale * jnp.dot(
            wide_rows, blocks_mat, preferred_element_type=jnp.float32
        )
        summed = lax.psum_scatter(
            jnp.concatenate([gate_term, up_product], axis=1), "tp", scatter_dimension=0, tiled=True
        )
        hidden = (jax.nn.silu(summed[:, :hidden_local]) * summed[:, hidden_local:]).astype(
            jnp.bfloat16
        )
        partial_out = jnp.dot(
            lax.all_gather(hidden, "tp", axis=0, tiled=True),
            down_matrix,
            preferred_element_type=jnp.float32,
        )
        out_total = by_axis(partial_out, POOL)
        outputs.append(out_total.astype(jnp.bfloat16).reshape(group_size, row_count, local_width))
    return jnp.concatenate(outputs, axis=0)


def solution(mesh):
    split = Mesh(mesh.devices.reshape(8, 4, mesh.shape["tp"]), ("pool_0", "pool_1", "tp"))
    return jax.shard_map(
        on_device,
        mesh=split,
        in_specs=(
            P(None, None, "tp"),
            P("tp", POOL),
            P("tp", POOL),
            P(POOL, "tp"),
            P(POOL, None, "tp"),
            P(POOL, "tp", None),
            P(),
            P(),
        ),
        out_specs=P(None, None, "tp"),
        check_vma=False,
    )
```

profile of v0, /device:TPU:48, one launch (start us, length us, event | category | flops | bytes accessed | tf_op | source)
XLA Modules:
  0.0 339.1 jit_solution(7243623281947806800)
XLA Ops:
  6.5 1.1 select_reduce_fusion
  7.7 1.3 fusion.2
  9.0 0.6 reshape.818
  9.6 8.6 %all-to-all-start = ((f32[16,256,4]{1,2,0:T(4,128)}), f32[16,256,4]{1,2,0:T(4,128)S(1)}, u32[]{:S(2)}, u32[]{:S(2)}) async-start(f32[16,256,4]{1,2,0:T(4,128)} %bitcast.7), calls=%async_computation | async-start | bytes 131072 | tf_op jit(solution)/shard_map/all_to_all | solution.py:23
  19.8 0.6 dynamic-slice.7
  20.4 0.6 dynamic-slice.9
  21.1 0.7 dynamic-slice.10
  21.9 0.6 dynamic-slice.8
  22.5 3.2 fusion.38
  30.8 2.3 fusion.10
  33.1 1.0 dynamic-slice_select_fusion.1
  34.1 0.7 broadcast_in_dim.130
  34.8 11.6 %all-to-all-start.1 = ((f32[32,256,4]{1,2,0:T(4,128)}), f32[32,256,4]{1,2,0:T(4,128)S(1)}, u32[]{:S(2)}, u32[]{:S(2)}) async-start(f32[32,256,4]{1,2,0:T(4,128)} %broadcast_in_dim.130), calls=%async_computation.1 | async-start | bytes 262144 | tf_op jit(solution)/shard_map/all_to_all | solution.py:29
  46.4 0.4 fusion.12
  46.9 10.3 %all-to-all-done.1 = f32[32,256,4]{1,2,0:T(4,128)S(1)} async-done(((f32[32,256,4]{1,2,0:T(4,128)}), f32[32,256,4]{1,2,0:T(4,128)S(1)}, u32[]{:S(2)}, u32[]{:S(2)}) %all-to-all-start.1) | async-done | bytes 131104 | tf_op jit(solution)/shard_map/all_to_all | solution.py:29
  57.2 0.7 copy-done.5
  57.8 3.9 %all-to-all-start.2 = ((bf16[1,4,32,896]{3,1,0,2:T(4,128)(2,1)}), bf16[1,4,32,896]{3,1,0,2:T(4,128)(2,1)S(1)}, u32[]{:S(2)}, u32[]{:S(2)}) async-start(bf16[1,4,32,896]{3,1,0,2:T(4,128)(2,1)} %bitcast.12), calls=%async_computation.2 | async-start | bytes 458752 | tf_op jit(solution)/shard_map/all_to_all | solution.py:99
  61.8 1.0 reduce_sum.108
  62.7 0.7 broadcast_select_fusion.1
  63.4 1.5 select_n.160
  64.9 8.2 %all-to-all-done.2 = bf16[1,4,32,896]{3,1,0,2:T(4,128)(2,1)S(1)} async-done(((bf16[1,4,32,896]{3,1,0,2:T(4,128)(2,1)}), bf16[1,4,32,896]{3,1,0,2:T(4,128)(2,1)S(1)}, u32[]{:S(2)}, u32[]{:S(2)}) %all-to-all-start.2) | async-done | bytes 229408 | tf_op jit(solution)/shard_map/all_to_all | solution.py:99
  73.1 0.7 copy-done.4
  73.8 1.0 reshape.821
  74.8 1.5 fusion.1
  76.3 1.4 pad_maximum_fusion
  77.8 0.9 copy-done.7
  78.9 0.7 reshape.825
  79.6 7.2 %all-to-all-start.3 = ((f32[16,256,4]{1,2,0:T(4,128)}), f32[16,256,4]{1,2,0:T(4,128)S(1)}, u32[]{:S(2)}, u32[]{:S(2)}) async-start(f32[16,256,4]{1,2,0:T(4,128)} %bitcast.23), calls=%async_computation.4 | async-start | bytes 131072 | tf_op jit(solution)/shard_map/all_to_all | solution.py:23
  86.8 1.4 fusion.5
  88.2 3.2 all-to-all-done.3
  91.4 0.7 broadcast_in_dim.136
  92.1 3.9 %all-to-all-start.4 = ((f32[32,256,4]{1,2,0:T(4,128)}), f32[32,256,4]{1,2,0:T(4,128)S(1)}, u32[]{:S(2)}, u32[]{:S(2)}) async-start(f32[32,256,4]{1,2,0:T(4,128)} %broadcast_in_dim.136), calls=%async_computation.5 | async-start | bytes 262144 | tf_op jit(solution)/shard_map/all_to_all | solution.py:29
  96.4 10.7 %all-to-all-done.4 = f32[32,256,4]{1,2,0:T(4,128)S(1)} async-done(((f32[32,256,4]{1,2,0:T(4,128)}), f32[32,256,4]{1,2,0:T(4,128)S(1)}, u32[]{:S(2)}, u32[]{:S(2)}) %all-to-all-start.4) | async-done | bytes 131104 | tf_op jit(solution)/shard_map/all_to_all | solution.py:29
  107.1 3.9 %all-to-all-start.5 = ((bf16[1,4,32,896]{3,1,0,2:T(4,128)(2,1)}), bf16[1,4,32,896]{3,1,0,2:T(4,128)(2,1)S(1)}, u32[]{:S(2)}, u32[]{:S(2)}) async-start(bf16[1,4,32,896]{3,1,0,2:T(4,128)(2,1)} %bitcast.28), calls=%async_computation.6 | async-start | bytes 458752 | tf_op jit(solution)/shard_map/all_to_all | solution.py:99
  111.1 11.5 %all-to-all-done.5 = bf16[1,4,32,896]{3,1,0,2:T(4,128)(2,1)S(1)} async-done(((bf16[1,4,32,896]{3,1,0,2:T(4,128)(2,1)}), bf16[1,4,32,896]{3,1,0,2:T(4,128)(2,1)S(1)}, u32[]{:S(2)}, u32[]{:S(2)}) %all-to-all-start.5) | async-done | bytes 229408 | tf_op jit(solution)/shard_map/all_to_all | solution.py:99
  122.7 1.5 fusion
  124.2 1.3 pad_maximum_fusion.1
  125.6 3.3 reduce-scatter.3.cloned.1.call-done
  128.9 0.9 fusion.23
  129.8 18.8 %all_gather.6 = bf16[256,896]{1,0:T(8,128)(2,1)S(1)} all-gather(bf16[16,896]{1,0:T(8,128)(2,1)S(1)} %fusion.23), channel_id=1, replica_groups=mesh['pool_0'=8,'pool_1'=4,'tp'=16] {'tp'}, dimensions={0}, use_global_device_ids=true | all-gather | bytes 487424 | tf_op jit(solution)/shard_map/all_gather | solution.py:127
  148.6 43.9 %reduce-scatter.5.cloned.1.call-done = f32[16,1792]{1,0:T(8,128)} async-done(((f32[256,1792]{1,0:T(8,128)}), f32[16,1792]{1,0:T(8,128)}) %reduce-scatter.5.cloned.1.call-update) | async-done | bytes 114704 | tf_op jit(solution)/shard_map/reduce_scatter | solution.py:120
  192.5 0.9 fusion.22
  193.4 18.8 %all_gather.7 = bf16[256,896]{1,0:T(8,128)(2,1)S(1)} all-gather(bf16[16,896]{1,0:T(8,128)(2,1)S(1)} %fusion.22), channel_id=1, replica_groups=mesh['pool_0'=8,'pool_1'=4,'tp'=16] {'tp'}, dimensions={0}, use_global_device_ids=true | all-gather | bytes 487424 | tf_op jit(solution)/shard_map/all_gather | solution.py:127
  212.2 1.3 fusion.41
  213.5 1.2 fusion.42
  214.7 84.6 %all-reduce.5.cloned.1.call-done = (f32[256,512]{1,0:T(8,128)}, f32[256,512]{1,0:T(8,128)}) async-done(((f32[256,512]{1,0:T(8,128)}, f32[256,512]{1,0:T(8,128)}), (f32[256,512]{1,0:T(8,128)}, f32[256,512]{1,0:T(8,128)})) %all-reduce.5.cloned.1.call-update) | async-done | bytes 1048592 | tf_op jit(solution)/shard_map/psum | solution.py:38
  299.4 32.3 %all-reduce.6 = (bf16[256,512]{1,0:T(8,128)(2,1)S(1)}, bf16[256,512]{1,0:T(8,128)(2,1)S(1)}) all-reduce(f32[256,512]{1,0:T(8,128)} %get-tuple-element.17, f32[256,512]{1,0:T(8,128)} %get-tuple-element.18), channel_id=1, replica_groups=mesh['pool_0'=8,'pool_1'=4,'tp'=16] {'pool_1'}, use_global_device_ids=true, to_apply=%region_20.22 | all-reduce | flops 262144 | bytes 1572864 | tf_op jit(solution)/shard_map/psum | solution.py:38
  331.7 0.8 pad_maximum_fusion.2
  (64 shorter events, 4.1 us)
Async XLA Ops:
  6.5 24.2 %copy-start = (bf16[512,896]{1,0:T(8,128)(2,1)S(1)}, bf16[512,896]{1,0:T(8,128)(2,1)}, u32[]{:S(2)}) copy-start(bf16[512,896]{1,0:T(8,128)(2,1)} %param.12) | copy-start | bytes 2752516
  6.5 26.6 %copy-start.6 = (bf16[4,4,28672]{2,1,0:T(4,128)(2,1)S(1)}, bf16[4,4,28672]{2,1,0:T(4,128)(2,1)}, u32[]{:S(2)}) copy-start(bf16[4,4,28672]{2,1,0:T(4,128)(2,1)} %param.15) | copy-start | bytes 2752516
  9.6 24.4 %all-to-all-start = ((f32[16,256,4]{1,2,0:T(4,128)}), f32[16,256,4]{1,2,0:T(4,128)S(1)}, u32[]{:S(2)}, u32[]{:S(2)}) async-start(f32[16,256,4]{1,2,0:T(4,128)} %bitcast.7), calls=%async_computation | async-start | bytes 131072 | tf_op jit(solution)/shard_map/all_to_all | solution.py:23
  26.9 19.5 %copy-start.1 = (bf16[512,896]{1,0:T(8,128)(2,1)S(1)}, bf16[512,896]{1,0:T(8,128)(2,1)}, u32[]{:S(2)}) copy-start(bf16[512,896]{1,0:T(8,128)(2,1)} %param.11) | copy-start | bytes 2752516
  26.9 19.5 %copy-start.3 = (bf16[2,256,512]{2,1,0:T(8,128)(2,1)S(1)}, bf16[2,256,512]{2,1,0:T(8,128)(2,1)}, u32[]{:S(2)}) copy-start(bf16[2,256,512]{2,1,0:T(8,128)(2,1)} %param.10) | copy-start | bytes 1572868
  34.8 22.4 %all-to-all-start.1 = ((f32[32,256,4]{1,2,0:T(4,128)}), f32[32,256,4]{1,2,0:T(4,128)S(1)}, u32[]{:S(2)}, u32[]{:S(2)}) async-start(f32[32,256,4]{1,2,0:T(4,128)} %broadcast_in_dim.130), calls=%async_computation.1 | async-start | bytes 262144 | tf_op jit(solution)/shard_map/all_to_all | solution.py:29
  57.2 0.7 copy-start.5
  57.8 15.3 %all-to-all-start.2 = ((bf16[1,4,32,896]{3,1,0,2:T(4,128)(2,1)}), bf16[1,4,32,896]{3,1,0,2:T(4,128)(2,1)S(1)}, u32[]{:S(2)}, u32[]{:S(2)}) async-start(bf16[1,4,32,896]{3,1,0,2:T(4,128)(2,1)} %bitcast.12), calls=%async_computation.2 | async-start | bytes 458752 | tf_op jit(solution)/shard_map/all_to_all | solution.py:99
  61.7 67.2 %reduce-scatter.3.cloned.1.call-start = ((), (), s32[]{:S(2)}) async-start(), calls=%async_computation.8 | async-start | bytes 1949696 | tf_op jit(solution)/shard_map/reduce_scatter | solution.py:120
  73.1 0.7 copy-start.4
  77.7 0.9 copy-start.7
  79.6 11.8 %all-to-all-start.3 = ((f32[16,256,4]{1,2,0:T(4,128)}), f32[16,256,4]{1,2,0:T(4,128)S(1)}, u32[]{:S(2)}, u32[]{:S(2)}) async-start(f32[16,256,4]{1,2,0:T(4,128)} %bitcast.23), calls=%async_computation.4 | async-start | bytes 131072 | tf_op jit(solution)/shard_map/all_to_all | solution.py:23
  92.1 15.0 %all-to-all-start.4 = ((f32[32,256,4]{1,2,0:T(4,128)}), f32[32,256,4]{1,2,0:T(4,128)S(1)}, u32[]{:S(2)}, u32[]{:S(2)}) async-start(f32[32,256,4]{1,2,0:T(4,128)} %broadcast_in_dim.136), calls=%async_computation.5 | async-start | bytes 262144 | tf_op jit(solution)/shard_map/all_to_all | solution.py:29
  107.1 15.6 %all-to-all-start.5 = ((bf16[1,4,32,896]{3,1,0,2:T(4,128)(2,1)}), bf16[1,4,32,896]{3,1,0,2:T(4,128)(2,1)S(1)}, u32[]{:S(2)}, u32[]{:S(2)}) async-start(bf16[1,4,32,896]{3,1,0,2:T(4,128)(2,1)} %bitcast.28), calls=%async_computation.6 | async-start | bytes 458752 | tf_op jit(solution)/shard_map/all_to_all | solution.py:99
  110.9 81.6 %reduce-scatter.5.cloned.1.call-start = ((), (), s32[]{:S(2)}) async-start(), calls=%async_computation.9 | async-start | bytes 1949696 | tf_op jit(solution)/shard_map/reduce_scatter | solution.py:120
  125.5 86.7 %copy-start.2 = (bf16[896,512]{1,0:T(8,128)(2,1)S(1)}, bf16[896,512]{1,0:T(8,128)(2,1)}, u32[]{:S(2)}) copy-start(bf16[896,512]{1,0:T(8,128)(2,1)} %param.13) | copy-start | bytes 2752516
  125.6 173.8 %all-reduce.5.cloned.1.call-start = ((), (), s32[]{:S(2)}) async-start(), calls=%async_computation.10 | async-start | bytes 2097152 | tf_op jit(solution)/shard_map/psum | solution.py:38
Sparse Core Ops, SparseCore 0:
  77.9 51.0 reduce-scatter.2
  131.8 60.7 reduce-scatter.4
  214.8 84.4 all-reduce.4
where the time goes:
time: 340 us; the launch traced here: 339 us
  waiting for transfers between devices  176 us (52%)
  blocking collectives  69.9 us (21%)
  starting transfers between devices  39.1 us (12%)
  between operations  17.3 us (5%)
  other arithmetic  14 us (4%)
  matrix products  11.6 us (3%)
  local copies, waits for them, and re-layouts  11.3 us (3%)
    psum x1, waiting for transfers between devices, by_axis(): return functools.reduce(lax.psum, axes, value)  84.6 us
    reduce_scatter x2, waiting for transfers between devices, on_device(): lax.psum_scatter(jnp.concatenate([gate_term, up_product], axis=1), 'tp',...  47.3 us
    all_gather x2, blocking collectives, on_device(): lax.all_gather(hidden, 'tp', axis=0, tiled=True)  37.6 us
    psum x1, blocking collectives, by_axis(): return functools.reduce(lax.psum, axes, value)  32.3 us
    all_to_all x2, waiting for transfers between devices, copy_for_each(): return lax.all_to_all(copies, axis, split_axis=0, concat_axis=0, tiled=True)  21 us
    all_to_all x2, waiting for transfers between devices, on_device(): lax.all_to_all(outgoing, POOL, split_axis=2, concat_axis=0, tiled=True)  19.7 us
    all_to_all x2, starting transfers between devices, sum_at_owner(): pieces = lax.all_to_all(in_blocks(value, dim, size), axis, 0, 0, tiled=True)  15.8 us
    all_to_all x2, starting transfers between devices, copy_for_each(): return lax.all_to_all(copies, axis, split_axis=0, concat_axis=0, tiled=True)  15.5 us
  transfers between devices with their start and end apart: 9, of which 8 were waited for; matrix products, arithmetic and copies ran while one was open for 7% of the time, Pallas kernels for 0%

commit v1 on v0

v1 whole, which is shorter than its diff:
```python
import functools

import jax
import jax.numpy as jnp
from jax import lax
from jax.experimental import pallas as pl
from jax.experimental.pallas import tpu as pltpu
from jax.sharding import PartitionSpec as P

MESH = pl.DeviceIdType.MESH
F32 = jnp.float32
BF16 = jnp.bfloat16
adapter_scale = 2.0

NY, NZ, NX = 8, 8, 4
NPOOL = NZ * NX


def mod(a, n):
    return lax.rem(a + n, n)


def remote(src, dst, ssem, rsem, device):
    return pltpu.make_async_remote_copy(
        src_ref=src, dst_ref=dst, send_sem=ssem, recv_sem=rsem, device_id=device, device_id_type=MESH
    )


def kernel(
    acts, gate, up, down, shrink, expand, rowad, ptab, out,
    abuf, gbuf, ubuf, dbuf, sbuf, ebuf, esel, epar, e8, blocks, wide, lrs, lrr, lr8,
    gacc, uacc, gpart, upart, grecv, urecv, hid, xs, xr, zs, zr, zg, obuf,
    lsem, psend, precv, esend, erecv, wsend, wrecv, lsend, lrecv, gsend, grsem, usend, ursem,
    hsend, hrecv, xsend, xrecv, zsend, zrecv, fsend, frecv, osend, orecv,
):
    rows, width = abuf.shape[1], abuf.shape[2]
    hidden = gbuf.shape[2]
    piece = rows // NY
    p = lax.axis_index("pool")
    t = lax.axis_index("tp")
    c = lax.rem(t, 2)
    o = 1 - c
    y = t // 2
    z = p // NX
    x = lax.rem(p, NX)
    partner = (p, 2 * y + o)

    def at_y(n):
        return (p, 2 * mod(y + n, NY) + c)

    def at_z(n):
        return (mod(z + n, NZ) * NX + x, t)

    def at_x(n):
        return (z * NX + mod(x + n, NX), t)

    bar = pltpu.get_barrier_semaphore()
    pl.semaphore_signal(bar, inc=1, device_id=partner, device_id_type=MESH)
    for n in range(1, NY):
        pl.semaphore_signal(bar, inc=1, device_id=at_y(n), device_id_type=MESH)

    def greet(n, carry):
        pl.semaphore_signal(bar, inc=1, device_id=(mod(p + n, NPOOL), t), device_id_type=MESH)
        return carry

    lax.fori_loop(1, NPOOL, greet, 0)
    for n in range(1, NX):
        pl.semaphore_signal(
            bar, inc=1, device_id=(z * NX + mod(x + n, NX), 2 * y + o), device_id_type=MESH
        )

    loads = [
        pltpu.make_async_copy(expand, ebuf, lsem.at[0]),
        pltpu.make_async_copy(acts.at[c], abuf.at[c], lsem.at[1]),
        pltpu.make_async_copy(shrink, sbuf.at[c], lsem.at[2]),
        pltpu.make_async_copy(gate, gbuf.at[c], lsem.at[3]),
        pltpu.make_async_copy(up, ubuf.at[c], lsem.at[4]),
        pltpu.make_async_copy(down, dbuf.at[c], lsem.at[5]),
    ]
    for cp in loads:
        cp.start()

    table = jnp.broadcast_to(ptab[...].astype(F32).astype(BF16), (8, ptab.shape[1]))
    base = (p * expand.shape[0]).astype(F32)
    rel = []
    for m in range(2):
        ids = jnp.broadcast_to(rowad[m : m + 1, :], (ptab.shape[1], rows))
        hot = (lax.broadcasted_iota(jnp.int32, ids.shape, 0) == ids).astype(F32).astype(BF16)
        rel.append(jnp.dot(table, hot, preferred_element_type=F32) - base)
    rel_mine = jnp.where(c == 0, rel[0], rel[1])
    rel_other = jnp.where(c == 0, rel[1], rel[0])
    pages = expand.shape[0]

    def used(r, j):
        return jnp.max(jnp.where(r == float(j), 1.0, 0.0), axis=1, keepdims=True)

    use_mine = [used(rel_mine, j) for j in range(pages)]
    use_other = [used(rel_other, j) for j in range(pages)]
    row_mask = (rel_mine[0:1, :] > -0.5) & (rel_mine[0:1, :] < pages - 0.5)

    loads[0].wait()
    chunk = 2048

    def pick(i, carry):
        cols = pl.ds(pl.multiple_of(i * chunk, chunk), chunk)
        mine = jnp.zeros((ebuf.shape[1], chunk), F32)
        other = jnp.zeros((ebuf.shape[1], chunk), F32)
        for j in range(pages):
            page = ebuf[j, :, cols].astype(F32)
            mine = mine + page * use_mine[j][:4]
            other = other + page * use_other[j][:4]
        esel[0, :, cols] = mine.astype(BF16)
        esel[1, :, cols] = other.astype(BF16)
        return carry

    lax.fori_loop(0, ebuf.shape[2] // chunk, pick, 0)

    for cp in loads[1:]:
        cp.wait()
    pl.semaphore_wait(bar, 1 + (NY - 1) + (NPOOL - 1) + (NX - 1))

    ex = [
        remote(esel.at[1], epar, psend.at[0], precv.at[0], partner),
        remote(acts.at[o], abuf.at[c], psend.at[1], precv.at[1], partner),
        remote(sbuf.at[c], sbuf.at[c], psend.at[2], precv.at[2], partner),
        remote(gbuf.at[c], gbuf.at[c], psend.at[3], precv.at[3], partner),
        remote(ubuf.at[c], ubuf.at[c], psend.at[4], precv.at[4], partner),
        remote(dbuf.at[c], dbuf.at[c], psend.at[5], precv.at[5], partner),
    ]
    for cp in ex:
        cp.start()

    gacc[...] = jnp.dot(abuf[c], gbuf[c], preferred_element_type=F32)
    uacc[...] = jnp.dot(abuf[c], ubuf[c], preferred_element_type=F32)

    ex[0].wait_recv()

    def join(i, carry):
        cols = pl.ds(pl.multiple_of(i * chunk, chunk), chunk)
        a = esel[0, :, cols].astype(F32)
        b = epar[:, cols].astype(F32)
        low = jnp.where(c == 0, a, b)
        high = jnp.where(c == 0, b, a)
        e8[:, cols] = jnp.concatenate([low, high], axis=0).astype(BF16)
        return carry

    lax.fori_loop(0, ebuf.shape[2] // chunk, join, 0)

    def block_to(n):
        q = mod(p + n, NPOOL)
        return remote(
            e8.at[:, pl.ds(pl.multiple_of(q * hidden, 128), hidden)],
            blocks.at[p],
            esend.at[n],
            erecv.at[p],
            (q, t),
        )

    def send_block(n, carry):
        block_to(n).start()
        return carry

    lax.fori_loop(1, NPOOL, send_block, 0)
    blocks[p] = e8[:, pl.ds(pl.multiple_of(p * hidden, 128), hidden)]

    ex[1].wait_recv()
    ex[2].wait_recv()
    low = jnp.zeros((sbuf.shape[2], rows), F32)
    for half in range(2):
        factor = jnp.zeros(sbuf.shape[2:], F32)
        for j in range(pages):
            factor = factor + sbuf[half, j].astype(F32) * use_mine[j][0:1]
        low = low + lax.dot_general(
            factor.astype(BF16), abuf[half], (((1,), (1,)), ((), ())), preferred_element_type=F32
        )
    low = jnp.where(row_mask, low, 0.0)
    for k in range(NY):
        lrs[k] = low[8 * k : 8 * k + 8, :]
    lcopy = []
    for n in range(1, NY):
        cp = remote(lrs.at[mod(y + n, NY)], lrr.at[n], lsend.at[n], lrecv.at[n], at_y(n))
        cp.start()
        lcopy.append(cp)

    ex[3].wait_recv()
    gacc[...] += jnp.dot(abuf[o], gbuf[o], preferred_element_type=F32)
    gpart[...] = gacc[...].astype(BF16).reshape(gpart.shape)
    gcopy = []
    for n in (4, 3, 5, 2, 6, 1, 7):
        cp = remote(gpart.at[mod(y + n, NY)], grecv.at[n], gsend.at[n], grsem.at[n], at_y(n))
        cp.start()
        gcopy.append(cp)

    total = lrs[y]
    for n in range(1, NY):
        lcopy[n - 1].wait_recv()
        total = total + lrr[n]
    lr8[...] = total.astype(BF16)

    def rank_to(n):
        q = mod(p + n, NPOOL)
        return remote(lr8, wide.at[p], wsend.at[n], wrecv.at[p], (q, t))

    def send_rank(n, carry):
        rank_to(n).start()
        return carry

    lax.fori_loop(1, NPOOL, send_rank, 0)
    wide[p] = lr8[...]

    ex[4].wait_recv()
    uacc[...] += jnp.dot(abuf[o], ubuf[o], preferred_element_type=F32)

    def arrived(n, carry):
        q = mod(p + n, NPOOL)
        remote(e8.at[:, pl.ds(0, hidden)], blocks.at[q], esend.at[n], erecv.at[q], (q, t)).wait_recv()
        remote(lr8, wide.at[q], wsend.at[n], wrecv.at[q], (q, t)).wait_recv()
        return carry

    lax.fori_loop(1, NPOOL, arrived, 0)
    wide_all = wide[...].reshape(NPOOL * 8, rows)
    block_all = blocks[...].reshape(NPOOL * 8, hidden)
    uacc[...] += adapter_scale * lax.dot_general(
        wide_all, block_all, (((0,), (0,)), ((), ())), preferred_element_type=F32
    )
    upart[...] = uacc[...].astype(BF16).reshape(upart.shape)
    ucopy = []
    for n in (4, 3, 5, 2, 6, 1, 7):
        cp = remote(upart.at[mod(y + n, NY)], urecv.at[n], usend.at[n], ursem.at[n], at_y(n))
        cp.start()
        ucopy.append(cp)

    mine = pl.ds(pl.multiple_of(y * piece, piece), piece)
    g = gacc[mine, :]
    for n in (7, 1, 6, 2, 5, 3, 4):
        remote(gpart.at[0], grecv.at[n], gsend.at[n], grsem.at[n], at_y(n)).wait_recv()
        g = g + grecv[n].astype(F32)
    act = g / (1.0 + jnp.exp(-g))
    u = uacc[mine, :]
    for n in (7, 1, 6, 2, 5, 3, 4):
        remote(upart.at[0], urecv.at[n], usend.at[n], ursem.at[n], at_y(n)).wait_recv()
        u = u + urecv[n].astype(F32)
    hid[0] = (act * u).astype(BF16)
    hcopy = []
    for n in (4, 3, 5, 2, 6, 1, 7):
        cp = remote(hid.at[0], hid.at[n], hsend.at[n], hrecv.at[n], at_y(n))
        cp.start()
        hcopy.append(cp)

    ex[5].wait_recv()
    order = (0, 7, 1, 6, 2, 5, 3, 4)
    cols = xs.shape[3]

    def down_piece(n):
        h = hid[n]
        for half in range(2):
            part = jnp.dot(h, dbuf[half], preferred_element_type=F32).astype(BF16)
            xs[n, 2 * half] = part[:, :cols]
            xs[n, 2 * half + 1] = part[:, cols:]
        for k in (2, 1, 3):
            remote(
                xs.at[n, mod(x + k, NX)], xr.at[n, k], xsend.at[n, k], xrecv.at[n, k], at_x(k)
            ).start()

    def x_done(n):
        total = xs[n, x].astype(F32)
        for k in (1, 2, 3):
            remote(xs.at[n, 0], xr.at[n, k], xsend.at[n, k], xrecv.at[n, k], at_x(k)).wait_recv()
            total = total + xr[n, k].astype(F32)
        zs[n] = total.astype(BF16)
        owner = mod(y - n + NY, NY)

        @pl.when(owner == z)
        def _():
            zr[z] = zs[n]

        @pl.when(owner != z)
        def _():
            remote(
                zs.at[n], zr.at[z], zsend.at[n], zrecv.at[z], (owner * NX + x, t)
            ).start()

    for i, n in enumerate(order):
        if n > 0:
            remote(hid.at[0], hid.at[n], hsend.at[n], hrecv.at[n], at_y(n)).wait_recv()
        down_piece(n)
        if i > 1:
            x_done(order[i - 2])
    x_done(order[-2])
    x_done(order[-1])

    total = zr[z].astype(F32)
    for k in range(1, NZ):
        q = mod(z + k, NZ)
        remote(zs.at[0], zr.at[q], zsend.at[0], zrecv.at[q], at_z(k)).wait_recv()
        total = total + zr[q].astype(F32)
    here = pl.ds(pl.multiple_of(z * piece, piece), piece)
    zg[here, :] = total.astype(BF16)
    for k in (4, 3, 5, 2, 6, 1, 7):
        remote(zg.at[here], zg.at[here], fsend.at[k], frecv.at[k], at_z(k)).start()
    for k in range(1, NZ):
        there = pl.ds(pl.multiple_of(mod(z - k + NZ, NZ) * piece, piece), piece)
        remote(zg.at[here], zg.at[there], fsend.at[k], frecv.at[k], at_z(k)).wait_recv()

    side = x // 2
    odd = lax.rem(x, 2)
    place = obuf.at[c, :, pl.ds(pl.multiple_of(odd * cols, cols), cols)]
    for k in (2, 1, 3):
        remote(
            zg, place, osend.at[k], orecv.at[odd, c], (z * NX + mod(x + k, NX), 2 * y + side)
        ).start()

    @pl.when(side != c)
    def _():
        remote(zg, place, osend.at[0], orecv.at[odd, c], partner).start()

    @pl.when(side == c)
    def _():
        obuf[c, :, pl.ds(pl.multiple_of(odd * cols, cols), cols)] = zg[...]

    for a in range(2):
        for m in range(2):

            @pl.when(jnp.logical_or(2 * c + a != x, m != c))
            def _():
                remote(
                    zg, obuf.at[m, :, a * cols : (a + 1) * cols], osend.at[0], orecv.at[a, m], partner
                ).wait_recv()

    final = pltpu.make_async_copy(obuf, out, lsem.at[6])
    final.start()

    for cp in ex:
        cp.wait_send()
    for cp in lcopy + gcopy + ucopy + hcopy:
        cp.wait_send()

    def left(n, carry):
        block_to(n).wait_send()
        rank_to(n).wait_send()
        return carry

    lax.fori_loop(1, NPOOL, left, 0)
    for n in range(NY):
        for k in range(1, NX):
            remote(xs.at[n, 0], xr.at[n, k], xsend.at[n, k], xrecv.at[n, k], at_x(k)).wait_send()

        @pl.when(mod(y - n + NY, NY) != z)
        def _():
            remote(zs.at[n], zr.at[0], zsend.at[n], zrecv.at[0], at_z(1)).wait_send()

    for k in range(1, NZ):
        remote(zg.at[here], zg.at[here], fsend.at[k], frecv.at[k], at_z(k)).wait_send()
    for k in range(1, NX):
        remote(zg, place, osend.at[k], orecv.at[odd, c], partner).wait_send()

    @pl.when(side != c)
    def _():
        remote(zg, place, osend.at[0], orecv.at[odd, c], partner).wait_send()

    final.wait()


def on_device(acts, gate, up, down, shrink, expand, row_adapter, page_table):
    batches, rows, width = acts.shape
    hidden = gate.shape[1]
    out_width = down.shape[1]
    pages, rank, _ = shrink.shape
    rank_local, ff = expand.shape[1:]
    piece = rows // NY
    cols = 2 * out_width // NX
    anyspec = pl.BlockSpec(memory_space=pl.ANY)
    vmem = pl.BlockSpec(memory_space=pltpu.VMEM)
    dma = pltpu.SemaphoreType.DMA
    scratch = [
        pltpu.VMEM((2, rows, width), BF16),
        pltpu.VMEM((2, width, hidden), BF16),
        pltpu.VMEM((2, width, hidden), BF16),
        pltpu.VMEM((2, hidden, out_width), BF16),
        pltpu.VMEM((2, pages, rank, width), BF16),
        pltpu.VMEM((pages, rank_local, ff), BF16),
        pltpu.VMEM((2, rank_local, ff), BF16),
        pltpu.VMEM((rank_local, ff), BF16),
        pltpu.VMEM((2 * rank_local, ff), BF16),
        pltpu.VMEM((NPOOL, 2 * rank_local, hidden), BF16),
        pltpu.VMEM((NPOOL, 2 * rank_local, rows), BF16),
        pltpu.VMEM((NY, 2 * rank_local, rows), F32),
        pltpu.VMEM((NY, 2 * rank_local, rows), F32),
        pltpu.VMEM((2 * rank_local, rows), BF16),
        pltpu.VMEM((rows, hidden), F32),
        pltpu.VMEM((rows, hidden), F32),
        pltpu.VMEM((NY, piece, hidden), BF16),
        pltpu.VMEM((NY, piece, hidden), BF16),
        pltpu.VMEM((NY, piece, hidden), BF16),
        pltpu.VMEM((NY, piece, hidden), BF16),
        pltpu.VMEM((NY, piece, hidden), BF16),
        pltpu.VMEM((NY, NX, piece, cols), BF16),
        pltpu.VMEM((NY, NX, piece, cols), BF16),
        pltpu.VMEM((NY, piece, cols), BF16),
        pltpu.VMEM((NZ, piece, cols), BF16),
        pltpu.VMEM((rows, cols), BF16),
        pltpu.VMEM((batches, rows, out_width), BF16),
        dma((8,)),
        dma((6,)), dma((6,)),
        dma((NPOOL,)), dma((NPOOL,)),
        dma((NPOOL,)), dma((NPOOL,)),
        dma((NY,)), dma((NY,)),
        dma((NY,)), dma((NY,)),
        dma((NY,)), dma((NY,)),
        dma((NY,)), dma((NY,)),
        dma((NY, NX)), dma((NY, NX)),
        dma((NY,)), dma((NZ,)),
        dma((NZ,)), dma((NZ,)),
        dma((NX,)), dma((2, 2)),
    ]
    return pl.pallas_call(
        kernel,
        out_shape=jax.ShapeDtypeStruct((batches, rows, out_width), BF16),
        in_specs=[anyspec] * 6 + [vmem] * 2,
        out_specs=anyspec,
        scratch_shapes=scratch,
        compiler_params=pltpu.CompilerParams(
            collective_id=0, has_side_effects=True, vmem_limit_bytes=56 * 2**20
        ),
        name="layer",
    )(acts, gate, up, down, shrink, expand, row_adapter, page_table.reshape(1, -1))


def solution(mesh):
    return jax.shard_map(
        on_device,
        mesh=mesh,
        in_specs=(
            P(None, None, "tp"),
            P("tp", "pool"),
            P("tp", "pool"),
            P("pool", "tp"),
            P("pool", None, "tp"),
            P("pool", "tp", None),
            P(),
            P(),
        ),
        out_specs=P(None, None, "tp"),
        check_vma=False,
    )
```

time: 340 us -> 91.5 us (0.27)
  the two profiles are of different devices: /device:TPU:48 before, /device:TPU:1 now
where the time goes in v1:
time: 91.5 us; the launch traced here: 91.3 us
  Pallas kernels  89.4 us (98%)
  local copies, waits for them, and re-layouts  1.87 us (2%)
    pallas_call x1, Pallas kernels, on_device(): pl.pallas_call(kernel, out_shape=jax.ShapeDtypeStruct((batches, rows, out...  89.4 us
    unnamed x1, local copies, waits for them, and re-layouts  1.87 us

profile of v1, /device:TPU:1, one launch (start us, length us, event | category | flops | bytes accessed | tf_op | source)
XLA Modules:
  0.0 91.3 jit_solution(14905732224474572787)
XLA Ops:
  0.0 89.4 %layer.1 = bf16[2,256,512]{2,1,0:T(8,128)(2,1)} custom-call(bf16[2,256,512]{2,1,0:T(8,128)(2,1)} %acts.1, bf16[512,896]{1,0:T(8,128)(2,1)} %gate.1, bf16[512,896]{1,0:T(8,128)(2,1)} %up.1, bf16[896,512]{1,0:T(8,128)(2,1)} %down.1, bf16[4,64,512]{2,1,0:T(8,128)(2,1)} %shrink.1, bf16[4,4,28672]{2,1,0:T(4,128)(2,1)} %expand.1, s32[2,256]{1,0:T(2,128)} %rowad.1, ...), custom_call_target="tpu_custom_call" | custom-call | tf_op jit(solution)/shard_map/layer/pallas_call | solution.py:416
  89.5 1.9 %copy.10 = bf16[2,256,512]{2,1,0:T(8,128)(2,1)} copy(bf16[2,256,512]{2,1,0:T(8,128)(2,1)} %layer.1) | data formatting | bytes 1048576

commit v2 on v1

v2 whole, which is shorter than its diff:
```python
import functools

import jax
import jax.numpy as jnp
from jax import lax
from jax.experimental import pallas as pl
from jax.experimental.pallas import tpu as pltpu
from jax.sharding import PartitionSpec as P

MESH = pl.DeviceIdType.MESH
F32 = jnp.float32
BF16 = jnp.bfloat16
adapter_scale = 2.0

NY, NZ, NX = 8, 8, 4
NPOOL = NZ * NX
FIRST, LAST = 6, 26
VMEM_LIMIT = 24 * 2**20


def mod(a, n):
    return lax.rem(a + n, n)


def remote(src, dst, ssem, rsem, device):
    return pltpu.make_async_remote_copy(
        src_ref=src, dst_ref=dst, send_sem=ssem, recv_sem=rsem, device_id=device, device_id_type=MESH
    )


def kernel(
    acts, gate, up, down, shrink, expand, row_ids, pages_at, out, rowad, ptab,
    aloc, apar, gown, gpar, uown, upar, dbuf, sbuf, ebuf, esel, epar, e8, blocks, wide,
    lroth, lrpar, lrs, lrr, lr8, lrx, lrz, gacc, uacc, gpart, upart, act,
    m4, m2, f3, f1, hid, xs, xr, zs, zr, zg, obuf,
    lsem, psend, precv, esend, erecv, lsend, lrecv, lxs, lxr, lzs, lzr, rsend, rrecv,
    hsend, hrecv, xsend, xrecv, zsend, zrecv, fsend, frecv, osend, orecv,
):
    rows = apar.shape[0]
    hidden = gown.shape[1]
    pages = expand.shape[0]
    piece = rows // NY
    part_rows = piece // 2
    half_rows = part_rows // 2
    p = lax.axis_index("pool")
    t = lax.axis_index("tp")
    c = lax.rem(t, 2)
    o = 1 - c
    y = t // 2
    z = p // NX
    x = lax.rem(p, NX)
    partner = (p, 2 * y + o)
    pending = []

    def go(src, dst, ssem, rsem, device):
        cp = remote(src, dst, ssem, rsem, device)
        cp.start()
        pending.append(cp)

    def come(src, dst, ssem, rsem):
        remote(src, dst, ssem, rsem, partner).wait_recv()

    def at_y(n):
        return (p, 2 * mod(y + n + NY, NY) + c)

    def at_z(n):
        return (mod(z + n, NZ) * NX + x, t)

    def at_x(n):
        return (z * NX + mod(x + n, NX), t)

    bar = pltpu.get_barrier_semaphore()

    def greet(n, carry):
        pl.semaphore_signal(bar, inc=1, device_id=(mod(p + n, NPOOL), t), device_id_type=MESH)
        return carry

    lax.fori_loop(1, NPOOL, greet, 0)
    for n in (4, 3, 5, 2, 6, 1, 7):
        pl.semaphore_signal(bar, inc=1, device_id=at_y(n), device_id_type=MESH)
    for n in range(1, NX):
        pl.semaphore_signal(
            bar, inc=1, device_id=(z * NX + mod(x + n, NX), 2 * y + o), device_id_type=MESH
        )
    pl.semaphore_signal(bar, inc=1, device_id=partner, device_id_type=MESH)

    loads = [
        pltpu.make_async_copy(shrink, sbuf, lsem.at[0]),
        pltpu.make_async_copy(acts, aloc, lsem.at[1]),
        pltpu.make_async_copy(expand, ebuf, lsem.at[2]),
        pltpu.make_async_copy(gate, gown, lsem.at[3]),
        pltpu.make_async_copy(up, uown, lsem.at[4]),
        pltpu.make_async_copy(down, dbuf.at[c], lsem.at[5]),
    ]
    small = [
        pltpu.make_async_copy(row_ids, rowad, lsem.at[6]),
        pltpu.make_async_copy(pages_at, ptab, lsem.at[7]),
    ]
    for cp in small:
        cp.start()
    for cp in loads:
        cp.start()

    for cp in small:
        cp.wait()
    table = jnp.broadcast_to(ptab[...].astype(F32).astype(BF16), (8, ptab.shape[1]))
    base = (p * pages).astype(F32)
    rel = []
    for m in range(2):
        ids = jnp.broadcast_to(rowad[m : m + 1, :], (ptab.shape[1], rows))
        hot = (lax.broadcasted_iota(jnp.int32, ids.shape, 0) == ids).astype(F32).astype(BF16)
        rel.append(jnp.dot(table, hot, preferred_element_type=F32) - base)
    rel_mine = jnp.where(c == 0, rel[0], rel[1])
    rel_other = jnp.where(c == 0, rel[1], rel[0])

    def used(r, j):
        return jnp.max(jnp.where(r == float(j), 1.0, 0.0), axis=1, keepdims=True)

    use_mine = [used(rel_mine, j) for j in range(pages)]
    use_other = [used(rel_other, j) for j in range(pages)]
    row_mask = (rel_mine[0:1, :] > -0.5) & (rel_mine[0:1, :] < pages - 0.5)

    loads[0].wait()
    loads[1].wait()

    def low_part(use, a):
        factor = jnp.zeros(sbuf.shape[1:], F32)
        for j in range(pages):
            factor = factor + sbuf[j].astype(F32) * use[j][0:1]
        return lax.dot_general(
            factor.astype(BF16), a, (((1,), (1,)), ((), ())), preferred_element_type=F32
        )

    low = low_part(use_mine, aloc[c])
    lroth[...] = low_part(use_other, aloc[o])

    loads[2].wait()
    chunk = 2048

    def pick(i, carry):
        cols = pl.ds(pl.multiple_of(i * chunk, chunk), chunk)
        mine = jnp.zeros((ebuf.shape[1], chunk), F32)
        other = jnp.zeros((ebuf.shape[1], chunk), F32)
        for j in range(pages):
            page = ebuf[j, :, cols].astype(F32)
            mine = mine + page * use_mine[j][:4]
            other = other + page * use_other[j][:4]
        esel[0, :, cols] = mine.astype(BF16)
        esel[1, :, cols] = other.astype(BF16)
        return carry

    lax.fori_loop(0, ebuf.shape[2] // chunk, pick, 0)

    for cp in loads[3:]:
        cp.wait()
    gacc[...] = jnp.dot(aloc[c], gown[...], preferred_element_type=F32)
    uacc[...] = jnp.dot(aloc[c], uown[...], preferred_element_type=F32)
    pl.semaphore_wait(bar, 1 + (NY - 1) + (NPOOL - 1) + (NX - 1))

    ex = [
        remote(lroth, lrpar, psend.at[0], precv.at[0], partner),
        remote(esel.at[1], epar, psend.at[1], precv.at[1], partner),
        remote(aloc.at[o], apar, psend.at[2], precv.at[2], partner),
        remote(gown, gpar, psend.at[3], precv.at[3], partner),
        remote(uown, upar, psend.at[4], precv.at[4], partner),
        remote(dbuf.at[c], dbuf.at[c], psend.at[5], precv.at[5], partner),
    ]
    for cp in ex:
        cp.start()

    ex[0].wait_recv()
    low = jnp.where(row_mask, low + lrpar[...], 0.0)
    for k in range(NY):
        lrs[k] = low[8 * k : 8 * k + 8, :]
    for n in (4, 3, 5, 2, 6, 1, 7):
        go(lrs.at[mod(y + n, NY)], lrr.at[n], lsend.at[n], lrecv.at[n], at_y(n))

    ex[1].wait_recv()

    def join(i, carry):
        cols = pl.ds(pl.multiple_of(i * chunk, chunk), chunk)
        a = esel[0, :, cols].astype(F32)
        b = epar[:, cols].astype(F32)
        e8[:, cols] = jnp.concatenate(
            [jnp.where(c == 0, a, b), jnp.where(c == 0, b, a)], axis=0
        ).astype(BF16)
        return carry

    lax.fori_loop(0, ebuf.shape[2] // chunk, join, 0)

    def block_to(n):
        q = mod(p + n, NPOOL)
        return remote(
            e8.at[:, pl.ds(pl.multiple_of(q * hidden, 128), hidden)],
            blocks.at[p],
            esend.at[n],
            erecv.at[p],
            (q, t),
        )

    def send_block(n, carry):
        block_to(n).start()
        return carry

    lax.fori_loop(FIRST, LAST, send_block, 0)
    blocks[p] = e8[:, pl.ds(pl.multiple_of(p * hidden, 128), hidden)]

    def own_rows(dest, first, count):
        return pl.ds(pl.multiple_of(dest * piece + first, 8), count)

    def spans(s, h):
        near = h * part_rows + s * half_rows
        far = h * part_rows + (1 - s) * half_rows
        return near, far

    def sum_first(q, part, h):
        for s in range(2):
            d = 1 - 2 * s
            near, far = spans(s, h)
            go(
                part.at[mod(y + 4, NY), near : near + half_rows],
                m4.at[q, s, h],
                rsend.at[q, 0, s, h],
                rrecv.at[q, 0, s, h],
                at_y(d),
            )
            go(
                part.at[mod(y + 2 * d + NY, NY), h * part_rows : (h + 1) * part_rows],
                m2.at[q, s, h],
                rsend.at[q, 1, s, h],
                rrecv.at[q, 1, s, h],
                at_y(d),
            )
        for s in range(2):
            d = 1 - 2 * s
            near, far = spans(s, h)
            go(
                part.at[mod(y + 3 * d + NY, NY), far : far + half_rows],
                f3.at[q, s, far : far + half_rows],
                rsend.at[q, 2, s, h],
                rrecv.at[q, 2, s, h],
                at_y(3 * d),
            )

    def sum_second(q, part, acc, h):
        for s in range(2):
            d = 1 - 2 * s
            near, far = spans(s, h)
            dest = mod(y + 3 * d + NY, NY)
            come(m4.at[q, s, h], m4.at[q, s, h], rsend.at[q, 0, s, h], rrecv.at[q, 0, s, h])
            part[dest, near : near + half_rows, :] = (
                acc[own_rows(dest, near, half_rows), :] + m4[q, s, h].astype(F32)
            ).astype(BF16)
            go(
                part.at[dest, near : near + half_rows],
                f3.at[q, s, near : near + half_rows],
                rsend.at[q, 3, s, h],
                rrecv.at[q, 3, s, h],
                at_y(3 * d),
            )
        for s in range(2):
            d = 1 - 2 * s
            dest = mod(y + d + NY, NY)
            come(m2.at[q, s, h], m2.at[q, s, h], rsend.at[q, 1, s, h], rrecv.at[q, 1, s, h])
            part[dest, h * part_rows : (h + 1) * part_rows, :] = (
                acc[own_rows(dest, h * part_rows, part_rows), :] + m2[q, s, h].astype(F32)
            ).astype(BF16)
            go(
                part.at[dest, h * part_rows : (h + 1) * part_rows],
                f1.at[q, s, h],
                rsend.at[q, 4, s, h],
                rrecv.at[q, 4, s, h],
                at_y(d),
            )

    def sum_last(q, acc, h):
        total = acc[own_rows(y, h * part_rows, part_rows), :]
        span = slice(h * part_rows, (h + 1) * part_rows)
        for s in range(2):
            near, far = spans(s, h)
            a = f3.at[q, s, far : far + half_rows]
            b = f3.at[q, s, near : near + half_rows]
            come(a, a, rsend.at[q, 2, s, h], rrecv.at[q, 2, s, h])
            come(b, b, rsend.at[q, 3, s, h], rrecv.at[q, 3, s, h])
            come(f1.at[q, s, h], f1.at[q, s, h], rsend.at[q, 4, s, h], rrecv.at[q, 4, s, h])
            total = total + f3[q, s, span, :].astype(F32) + f1[q, s, h].astype(F32)
        return total

    ex[2].wait_recv()
    ex[3].wait_recv()
    gacc[...] += jnp.dot(apar[...], gpar[...], preferred_element_type=F32)
    gpart[...] = gacc[...].astype(BF16).reshape(gpart.shape)
    for h in range(2):
        sum_first(0, gpart, h)

    total = lrs[y]
    for n in range(1, NY):
        come(lrs.at[0], lrr.at[n], lsend.at[n], lrecv.at[n])
        total = total + lrr[n]
    lr8[0] = total.astype(BF16)
    for k in (2, 1, 3):
        go(lr8.at[0], lrx.at[k], lxs.at[k], lxr.at[k], at_x(k))

    for h in range(2):
        sum_second(0, gpart, gacc, h)

    total = lr8[0].astype(F32)
    for k in range(1, NX):
        come(lr8.at[0], lrx.at[k], lxs.at[k], lxr.at[k])
        total = total + lrx[k].astype(F32)
    lr8[1] = total.astype(BF16)
    for k in (4, 3, 5, 2, 6, 1, 7):
        go(lr8.at[1], lrz.at[k], lzs.at[k], lzr.at[k], at_z(k))
    lax.fori_loop(1, FIRST, send_block, 0)
    lax.fori_loop(LAST, NPOOL, send_block, 0)

    ex[4].wait_recv()
    uacc[...] += jnp.dot(apar[...], upar[...], preferred_element_type=F32)

    total = lr8[1].astype(F32)
    for k in range(1, NZ):
        come(lr8.at[1], lrz.at[k], lzs.at[k], lzr.at[k])
        total = total + lrz[k].astype(F32)
    page = rel_mine + base
    for q in range(NPOOL):
        owned = (page > q * pages - 0.5) & (page < (q + 1) * pages - 0.5)
        wide[q] = jnp.where(owned, total, 0.0).astype(BF16)

    for h in range(2):
        g = sum_last(0, gacc, h)
        act[h * part_rows : (h + 1) * part_rows, :] = g / (1.0 + jnp.exp(-g))

    def arrived(n, carry):
        q = mod(p + n, NPOOL)
        remote(e8.at[:, pl.ds(0, hidden)], blocks.at[q], esend.at[n], erecv.at[q], (q, t)).wait_recv()
        return carry

    lax.fori_loop(1, NPOOL, arrived, 0)
    wide_all = wide[...].reshape(NPOOL * 8, rows)
    block_all = blocks[...].reshape(NPOOL * 8, hidden)
    uacc[...] += adapter_scale * lax.dot_general(
        wide_all, block_all, (((0,), (0,)), ((), ())), preferred_element_type=F32
    )
    upart[...] = uacc[...].astype(BF16).reshape(upart.shape)
    for h in range(2):
        sum_first(1, upart, h)
    for h in range(2):
        sum_second(1, upart, uacc, h)

    def share_first(h):
        span = slice(h * part_rows, (h + 1) * part_rows)
        hid[0, span, :] = (act[span, :] * sum_last(1, uacc, h)).astype(BF16)
        for s in range(2):
            d = 1 - 2 * s
            one, three = (1, 3) if s == 0 else (7, 5)
            go(
                hid.at[0, span], hid.at[one, span],
                hsend.at[0, s, h], hrecv.at[0, s, h], at_y(d),
            )
            go(
                hid.at[0, span], hid.at[three, span],
                hsend.at[1, s, h], hrecv.at[1, s, h], at_y(3 * d),
            )

    def share_second(h):
        span = slice(h * part_rows, (h + 1) * part_rows)
        for s in range(2):
            d = 1 - 2 * s
            one, two = (1, 2) if s == 0 else (7, 6)
            come(hid.at[one, span], hid.at[one, span], hsend.at[0, s, h], hrecv.at[0, s, h])
            go(
                hid.at[one, span], hid.at[two, span],
                hsend.at[2, s, h], hrecv.at[2, s, h], at_y(d),
            )
        for s in range(2):
            d = 1 - 2 * s
            three = 3 if s == 0 else 5
            near, far = spans(s, h)
            come(hid.at[three, span], hid.at[three, span], hsend.at[1, s, h], hrecv.at[1, s, h])
            go(
                hid.at[three, near : near + half_rows], hid.at[4, near : near + half_rows],
                hsend.at[3, s, h], hrecv.at[3, s, h], at_y(d),
            )

    def shared(n):
        for h in range(2):
            span = slice(h * part_rows, (h + 1) * part_rows)
            if n in (2, 6):
                s = 0 if n == 2 else 1
                come(hid.at[n, span], hid.at[n, span], hsend.at[2, s, h], hrecv.at[2, s, h])
            if n == 4:
                for s in range(2):
                    near, far = spans(s, h)
                    v = hid.at[4, near : near + half_rows]
                    come(v, v, hsend.at[3, s, h], hrecv.at[3, s, h])

    for h in range(2):
        share_first(h)

    ex[5].wait_recv()
    cols = xs.shape[3]

    def down_piece(n):
        shared(n)
        for half in range(2):
            part = jnp.dot(hid[n], dbuf[half], preferred_element_type=F32).astype(BF16)
            xs[n, 2 * half] = part[:, :cols]
            xs[n, 2 * half + 1] = part[:, cols:]
        for k in (2, 1, 3):
            go(xs.at[n, mod(x + k, NX)], xr.at[n, k], xsend.at[n, k], xrecv.at[n, k], at_x(k))

    def x_done(n):
        total = xs[n, x].astype(F32)
        for k in (1, 2, 3):
            come(xs.at[n, 0], xr.at[n, k], xsend.at[n, k], xrecv.at[n, k])
            total = total + xr[n, k].astype(F32)
        zs[n] = total.astype(BF16)
        owner = mod(y - n + NY, NY)

        @pl.when(owner == z)
        def _():
            zr[z] = zs[n]

        @pl.when(owner != z)
        def _():
            remote(zs.at[n], zr.at[z], zsend.at[n], zrecv.at[z], (owner * NX + x, t)).start()

    down_piece(0)
    for h in range(2):
        share_second(h)
    order = (0, 1, 7, 3, 5, 2, 6, 4)
    for i, n in enumerate(order):
        if n > 0:
            down_piece(n)
        if i > 1:
            x_done(order[i - 2])
    x_done(order[-2])
    x_done(order[-1])

    total = zr[z].astype(F32)
    for k in range(1, NZ):
        q = mod(z + k, NZ)
        come(zs.at[0], zr.at[q], zsend.at[0], zrecv.at[q])
        total = total + zr[q].astype(F32)

    def block_rows(k):
        return pl.ds(pl.multiple_of(mod(z - k + NZ, NZ) * piece, piece), piece)

    here = block_rows(0)
    zg[here, :] = total.astype(BF16)
    for k in (4, 3, 5, 2, 6, 1, 7):
        go(zg.at[here], zg.at[here], fsend.at[k], frecv.at[k], at_z(k))

    side = x // 2
    odd = lax.rem(x, 2)
    place = pl.ds(pl.multiple_of(odd * cols, cols), cols)
    for k in (0, 1, 7, 2, 6, 3, 5, 4):
        there = block_rows(k)
        if k > 0:
            come(zg.at[here], zg.at[there], fsend.at[k], frecv.at[k])
        slot = mod(z - k + NZ, NZ)
        for n in (2, 1, 3):
            go(
                zg.at[there],
                obuf.at[c, there, place],
                osend.at[k, n],
                orecv.at[odd, c, slot],
                (z * NX + mod(x + n, NX), 2 * y + side),
            )

        @pl.when(side != c)
        def _():
            remote(
                zg.at[there], obuf.at[c, there, place], osend.at[k, 0], orecv.at[odd, c, slot], partner
            ).start()

        @pl.when(side == c)
        def _():
            obuf[c, there, place] = zg[there, :]

    for a in range(2):
        for m in range(2):

            @pl.when(jnp.logical_or(2 * c + a != x, m != c))
            def _():
                for k in range(NZ):
                    v = obuf.at[m, k * piece : (k + 1) * piece, a * cols : (a + 1) * cols]
                    come(v, v, osend.at[0, 0], orecv.at[a, m, k])

    final = pltpu.make_async_copy(obuf, out, lsem.at[8])
    final.start()

    for cp in ex + pending:
        cp.wait_send()

    def left(n, carry):
        block_to(n).wait_send()
        return carry

    lax.fori_loop(1, NPOOL, left, 0)
    for n in range(NY):

        @pl.when(mod(y - n + NY, NY) != z)
        def _():
            remote(zs.at[n], zr.at[0], zsend.at[n], zrecv.at[0], at_z(1)).wait_send()

    @pl.when(side != c)
    def _():
        for k in range(NZ):
            remote(
                zg.at[here], obuf.at[c, here, place], osend.at[k, 0], orecv.at[0, 0, 0], partner
            ).wait_send()

    final.wait()


def on_device(acts, gate, up, down, shrink, expand, row_adapter, page_table):
    batches, rows, width = acts.shape
    hidden = gate.shape[1]
    out_width = down.shape[1]
    pages, rank, _ = shrink.shape
    rank_local, ff = expand.shape[1:]
    piece = rows // NY
    cols = 2 * out_width // NX
    anyspec = pl.BlockSpec(memory_space=pl.ANY)
    dma = pltpu.SemaphoreType.DMA
    ranks = 2 * rank_local
    scratch = [
        pltpu.VMEM(row_adapter.shape, jnp.int32),
        pltpu.VMEM((1, page_table.shape[0]), jnp.int32),
        pltpu.VMEM((2, rows, width), BF16),
        pltpu.VMEM((rows, width), BF16),
        pltpu.VMEM((width, hidden), BF16),
        pltpu.VMEM((width, hidden), BF16),
        pltpu.VMEM((width, hidden), BF16),
        pltpu.VMEM((width, hidden), BF16),
        pltpu.VMEM((2, hidden, out_width), BF16),
        pltpu.VMEM((pages, rank, width), BF16),
        pltpu.VMEM((pages, rank_local, ff), BF16),
        pltpu.VMEM((2, rank_local, ff), BF16),
        pltpu.VMEM((rank_local, ff), BF16),
        pltpu.VMEM((ranks, ff), BF16),
        pltpu.VMEM((NPOOL, ranks, hidden), BF16),
        pltpu.VMEM((NPOOL, ranks, rows), BF16),
        pltpu.VMEM((rank, rows), F32),
        pltpu.VMEM((rank, rows), F32),
        pltpu.VMEM((NY, ranks, rows), F32),
        pltpu.VMEM((NY, ranks, rows), F32),
        pltpu.VMEM((2, ranks, rows), BF16),
        pltpu.VMEM((NX, ranks, rows), BF16),
        pltpu.VMEM((NZ, ranks, rows), BF16),
        pltpu.VMEM((rows, hidden), F32),
        pltpu.VMEM((rows, hidden), F32),
        pltpu.VMEM((NY, piece, hidden), BF16),
        pltpu.VMEM((NY, piece, hidden), BF16),
        pltpu.VMEM((piece, hidden), F32),
        pltpu.VMEM((2, 2, 2, piece // 4, hidden), BF16),
        pltpu.VMEM((2, 2, 2, piece // 2, hidden), BF16),
        pltpu.VMEM((2, 2, piece, hidden), BF16),
        pltpu.VMEM((2, 2, 2, piece // 2, hidden), BF16),
        pltpu.VMEM((NY, piece, hidden), BF16),
        pltpu.VMEM((NY, NX, piece, cols), BF16),
        pltpu.VMEM((NY, NX, piece, cols), BF16),
        pltpu.VMEM((NY, piece, cols), BF16),
        pltpu.VMEM((NZ, piece, cols), BF16),
        pltpu.VMEM((rows, cols), BF16),
        pltpu.VMEM((batches, rows, out_width), BF16),
        dma((9,)),
        dma((6,)), dma((6,)),
        dma((NPOOL,)), dma((NPOOL,)),
        dma((NY,)), dma((NY,)),
        dma((NX,)), dma((NX,)),
        dma((NZ,)), dma((NZ,)),
        dma((2, 5, 2, 2)), dma((2, 5, 2, 2)),
        dma((4, 2, 2)), dma((4, 2, 2)),
        dma((NY, NX)), dma((NY, NX)),
        dma((NY,)), dma((NZ,)),
        dma((NZ,)), dma((NZ,)),
        dma((NZ, NX)), dma((2, 2, NZ)),
    ]
    return pl.pallas_call(
        kernel,
        out_shape=jax.ShapeDtypeStruct((batches, rows, out_width), BF16),
        in_specs=[anyspec] * 8,
        out_specs=anyspec,
        scratch_shapes=scratch,
        compiler_params=pltpu.CompilerParams(
            collective_id=0, has_side_effects=True, vmem_limit_bytes=VMEM_LIMIT
        ),
        name="layer",
    )(*[pltpu.with_memory_space_constraint(v, pltpu.HBM) for v in (acts, gate, up, down, shrink, expand, row_adapter, page_table.reshape(1, -1))])


def solution(mesh):
    return jax.shard_map(
        on_device,
        mesh=mesh,
        in_specs=(
            P(None, None, "tp"),
            P("tp", "pool"),
            P("tp", "pool"),
            P("pool", "tp"),
            P("pool", None, "tp"),
            P("pool", "tp", None),
            P(),
            P(),
        ),
        out_specs=P(None, None, "tp"),
        check_vma=False,
    )
```

time: 91.5 us -> 79.2 us (0.87)
  Pallas kernels: 89.4 us -> 78.3 us
  local copies, waits for them, and re-layouts: 1.87 us -> 0.8 us
    pallas_call x1, Pallas kernels: 89.4 us -> 78.3 us  [on_device(): pl.pallas_call(kernel, out_shape=jax.ShapeDtypeStruct((batches, rows, out...]
    unnamed x1, local copies, waits for them, and re-layouts: 1.87 us -> 0.8 us
where the time goes in v2:
time: 79.2 us; the launch traced here: 79.1 us
  Pallas kernels  78.3 us (99%)
  local copies, waits for them, and re-layouts  0.8 us (1%)
    pallas_call x1, Pallas kernels, on_device(): pl.pallas_call(kernel, out_shape=jax.ShapeDtypeStruct((batches, rows, out...  78.3 us

profile of v2, /device:TPU:1, one launch (start us, length us, event | category | flops | bytes accessed | tf_op | source)
XLA Modules:
  0.0 79.1 jit_solution(834151033058727355)
XLA Ops:
  0.0 78.3 %layer.1 = bf16[2,256,512]{2,1,0:T(8,128)(2,1)S(1)} custom-call(bf16[2,256,512]{2,1,0:T(8,128)(2,1)} %acts.1, bf16[512,896]{1,0:T(8,128)(2,1)} %gate.1, bf16[512,896]{1,0:T(8,128)(2,1)} %up.1, bf16[896,512]{1,0:T(8,128)(2,1)} %down.1, bf16[4,64,512]{2,1,0:T(8,128)(2,1)} %shrink.1, bf16[4,4,28672]{2,1,0:T(4,128)(2,1)} %expand.1, s32[2,256]{1,0:T(2,128)} %row_ids.1, ...), custom_call_target="tpu_custom_call" | custom-call | tf_op jit(solution)/shard_map/layer/pallas_call | solution.py:581
  78.3 0.8 %copy.10 = bf16[2,256,512]{2,1,0:T(8,128)(2,1)} copy(bf16[2,256,512]{2,1,0:T(8,128)(2,1)S(1)} %layer.1) | data formatting | bytes 1048576

commit v3 on v2

--- a/solution.py
+++ b/solution.py
@@ -231,6 +231,8 @@
                 rrecv.at[q, 1, s, h],
                 at_y(d),
             )
+
+    def sum_direct(q, part, h):
         for s in range(2):
             d = 1 - 2 * s
             near, far = spans(s, h)
@@ -292,6 +294,8 @@
     gpart[...] = gacc[...].astype(BF16).reshape(gpart.shape)
     for h in range(2):
         sum_first(0, gpart, h)
+    for h in range(2):
+        sum_direct(0, gpart, h)
 
     total = lrs[y]
     for n in range(1, NY):
@@ -345,6 +349,8 @@
     for h in range(2):
         sum_first(1, upart, h)
     for h in range(2):
+        sum_direct(1, upart, h)
+    for h in range(2):
         sum_second(1, upart, uacc, h)
 
     def share_first(h):
@@ -362,7 +368,7 @@
                 hsend.at[1, s, h], hrecv.at[1, s, h], at_y(3 * d),
             )
 
-    def share_second(h):
+    def share_near(h):
         span = slice(h * part_rows, (h + 1) * part_rows)
         for s in range(2):
             d = 1 - 2 * s
@@ -372,6 +378,9 @@
                 hid.at[one, span], hid.at[two, span],
                 hsend.at[2, s, h], hrecv.at[2, s, h], at_y(d),
             )
+
+    def share_far(h):
+        span = slice(h * part_rows, (h + 1) * part_rows)
         for s in range(2):
             d = 1 - 2 * s
             three = 3 if s == 0 else 5
@@ -427,15 +436,18 @@
 
     down_piece(0)
     for h in range(2):
-        share_second(h)
+        share_near(h)
     order = (0, 1, 7, 3, 5, 2, 6, 4)
     for i, n in enumerate(order):
         if n > 0:
             down_piece(n)
-        if i > 1:
-            x_done(order[i - 2])
-    x_done(order[-2])
-    x_done(order[-1])
+        if n == 7:
+            for h in range(2):
+                share_far(h)
+        if i >= 7:
+            x_done(order[i - 7])
+    for n in order[-7:]:
+        x_done(n)
 
     total = zr[z].astype(F32)
     for k in range(1, NZ):

time: 79.2 us -> 73.9 us (0.933)
  Pallas kernels: 78.3 us -> 73 us
    pallas_call x1, Pallas kernels: 78.3 us -> 73 us  [on_device(): pl.pallas_call(kernel, out_shape=jax.ShapeDtypeStruct((batches, rows, out...]
where the time goes in v3:
time: 73.9 us; the launch traced here: 73.8 us
  Pallas kernels  73 us (99%)
  local copies, waits for them, and re-layouts  0.8 us (1%)
    pallas_call x1, Pallas kernels, on_device(): pl.pallas_call(kernel, out_shape=jax.ShapeDtypeStruct((batches, rows, out...  73 us

profile of v3, /device:TPU:1, one launch (start us, length us, event | category | flops | bytes accessed | tf_op | source)
XLA Modules:
  0.0 73.8 jit_solution(18436257523116495962)
XLA Ops:
  0.0 73.0 %layer.1 = bf16[2,256,512]{2,1,0:T(8,128)(2,1)S(1)} custom-call(bf16[2,256,512]{2,1,0:T(8,128)(2,1)} %acts.1, bf16[512,896]{1,0:T(8,128)(2,1)} %gate.1, bf16[512,896]{1,0:T(8,128)(2,1)} %up.1, bf16[896,512]{1,0:T(8,128)(2,1)} %down.1, bf16[4,64,512]{2,1,0:T(8,128)(2,1)} %shrink.1, bf16[4,4,28672]{2,1,0:T(4,128)(2,1)} %expand.1, s32[2,256]{1,0:T(2,128)} %row_ids.1, ...), custom_call_target="tpu_custom_call" | custom-call | tf_op jit(solution)/shard_map/layer/pallas_call | solution.py:593
  73.0 0.8 %copy.10 = bf16[2,256,512]{2,1,0:T(8,128)(2,1)} copy(bf16[2,256,512]{2,1,0:T(8,128)(2,1)S(1)} %layer.1) | data formatting | bytes 1048576

commit v4 on v3

--- a/solution.py
+++ b/solution.py
@@ -305,9 +305,6 @@
     for k in (2, 1, 3):
         go(lr8.at[0], lrx.at[k], lxs.at[k], lxr.at[k], at_x(k))
 
-    for h in range(2):
-        sum_second(0, gpart, gacc, h)
-
     total = lr8[0].astype(F32)
     for k in range(1, NX):
         come(lr8.at[0], lrx.at[k], lxs.at[k], lxr.at[k])
@@ -317,6 +314,9 @@
         go(lr8.at[1], lrz.at[k], lzs.at[k], lzr.at[k], at_z(k))
     lax.fori_loop(1, FIRST, send_block, 0)
     lax.fori_loop(LAST, NPOOL, send_block, 0)
+
+    for h in range(2):
+        sum_second(0, gpart, gacc, h)
 
     ex[4].wait_recv()
     uacc[...] += jnp.dot(apar[...], upar[...], preferred_element_type=F32)

time: 73.9 us -> 73.9 us (level)
  no operation moved by 1% of the time
where the time goes in v4:
time: 73.9 us; the launch traced here: 73.8 us
  Pallas kernels  73 us (99%)
  local copies, waits for them, and re-layouts  0.8 us (1%)
    pallas_call x1, Pallas kernels, on_device(): pl.pallas_call(kernel, out_shape=jax.ShapeDtypeStruct((batches, rows, out...  73 us

profile of v4, /device:TPU:1, one launch (start us, length us, event | category | flops | bytes accessed | tf_op | source)
XLA Modules:
  0.0 73.8 jit_solution(13774831742479465261)
XLA Ops:
  0.0 73.0 %layer.1 = bf16[2,256,512]{2,1,0:T(8,128)(2,1)S(1)} custom-call(bf16[2,256,512]{2,1,0:T(8,128)(2,1)} %acts.1, bf16[512,896]{1,0:T(8,128)(2,1)} %gate.1, bf16[512,896]{1,0:T(8,128)(2,1)} %up.1, bf16[896,512]{1,0:T(8,128)(2,1)} %down.1, bf16[4,64,512]{2,1,0:T(8,128)(2,1)} %shrink.1, bf16[4,4,28672]{2,1,0:T(4,128)(2,1)} %expand.1, s32[2,256]{1,0:T(2,128)} %row_ids.1, ...), custom_call_target="tpu_custom_call" | custom-call | tf_op jit(solution)/shard_map/layer/pallas_call | solution.py:593
  73.0 0.8 %copy.10 = bf16[2,256,512]{2,1,0:T(8,128)(2,1)} copy(bf16[2,256,512]{2,1,0:T(8,128)(2,1)S(1)} %layer.1) | data formatting | bytes 1048576
